TPU v7x, 32 devices: a whole 2x2x4 slice. The times are simulated.
32 devices in a mesh: groups: 2 (over x), hour: 16 (over z, y, core).
Axes of the slice: x: 2, y: 2, z: 4, core: 2. Of those that a mesh axis runs over, the one named last changes fastest.
Arguments:
- power: float32 [32, 16, 2048], P('groups', 'hour'), parts along dimension 0, may hold values from -3 to 3
- capacity: float32 [4096], P(('groups', 'hour')), parts along dimension 0, may hold values from 0.01 to 20
- flow_dual: float32 [32, 16, 4096], P('groups', 'hour'), parts along dimension 0, may hold values from -3 to 3
- upper_dual: float32 [32, 16, 2048], P('groups', 'hour'), parts along dimension 0, may hold values from 0 to 0.1
- lower_dual: float32 [32, 16, 2048], P('groups', 'hour'), parts along dimension 0, may hold values from 0 to 0.1
- price: float32 [32, 16], P('groups', 'hour'), parts along dimension 0, may hold values from -5 to 5
- load: bfloat16 [32, 16, 512], P('groups', 'hour'), parts along dimension 0, may hold values from -5 to 5
- shift_factors: bfloat16 [4096, 512], replicated, may hold values from -0.25 to 0.25
- line_limit: float32 [4096], replicated, may hold values from 0.5 to 3
- unit_bus: int32 [2048], replicated, may hold values from 0 to 511
- leakage: float32 [2048], replicated, may hold values from 0.015625 to 0.0625
- initial_state: float32 [4096], P('groups'), parts along dimension 0, may hold values from 0 to 10
- power_limit: float32 [2048], replicated, may hold values from 0.5 to 1.5
- capacity_cost: float32 [2048], replicated, may hold values from 0 to 0.1
Outputs:
- new_power: float32 [32, 16, 2048], P('groups', 'hour'), parts along dimension 0
- new_capacity: float32 [4096], P(('groups', 'hour')), parts along dimension 0
- new_flow_dual: float32 [32, 16, 4096], P('groups', 'hour'), parts along dimension 0
- new_upper_dual: float32 [32, 16, 2048], P('groups', 'hour'), parts along dimension 0
- new_lower_dual: float32 [32, 16, 2048], P('groups', 'hour'), parts along dimension 0
There are 2 independent parts, one for each index of `groups`. A program takes and returns all parts, laid end to end along the dimension named above; an argument that names none is the same for every part. Nothing has to cross between parts.
All inputs are finite; a program needn't handle non-finite values.
Results may differ from a plain program's by a relative error of at most 0.00093.
Values sent between devices are 32-bit elements; how exact they have to be, the bound alone decides.
A program may use at most 128 MiB of HBM per device.

v0:
```python
import functools

import jax
import jax.numpy as jnp
from jax import lax
from jax.experimental import pallas as pl
from jax.experimental.pallas import tpu as pltpu
from jax.sharding import PartitionSpec as P

ITERS = 4

primal_step = 0.05
dual_step = 0.01


def kernel(
    n,
    power_in,
    capacity_in,
    flow_in,
    upper_in,
    lower_in,
    price_in,
    load_in,
    shift_in,
    limit_in,
    bus_in,
    leak_in,
    start_in,
    plimit_in,
    cost_in,
    power_out,
    capacity_out,
    flow_out,
    upper_out,
    lower_out,
    shift,
    inc,
    power,
    grid,
    flow,
    bar16,
    upper,
    lower,
    upper_stage,
    lower_stage,
    adj,
    adj_got,
    bar,
    bar_got,
    send_sems,
    recv_sems,
    shift_sem,
):
    me = lax.axis_index("hour")
    scen, hdev, units = power_in.shape
    lines, buses = shift.shape
    ud = units // n
    hours = hdev * n
    load_shift = pltpu.make_async_copy(shift_in, shift, shift_sem)
    load_shift.start()

    def peer_of(k):
        return lax.rem(me + k, n)

    def from_of(k):
        return lax.rem(me + n - k, n)

    def copy_to(src, dst, channel, peer):
        return pltpu.make_async_remote_copy(
            src_ref=src.at[peer],
            dst_ref=dst.at[me],
            send_sem=send_sems.at[channel, peer],
            recv_sem=recv_sems.at[channel, me],
            device_id={"hour": peer},
            device_id_type=pl.DeviceIdType.MESH,
        )

    def wait_from(dst, channel, source):
        pltpu.make_async_remote_copy(
            src_ref=dst.at[source],
            dst_ref=dst.at[source],
            send_sem=send_sems.at[channel, source],
            recv_sem=recv_sems.at[channel, source],
            device_id={"hour": source},
            device_id_type=pl.DeviceIdType.MESH,
        ).wait_recv()

    def each(count_from, function):
        def step(k, carry):
            function(k)
            return carry

        lax.fori_loop(count_from, n, step, 0)

    def rows_of(ref, lanes):
        return jnp.concatenate([ref[:, j, lanes] for j in range(hdev)], axis=0)

    barrier = pltpu.get_barrier_semaphore()
    each(
        1,
        lambda k: pl.semaphore_signal(
            barrier,
            inc=1,
            device_id={"hour": peer_of(k)},
            device_id_type=pl.DeviceIdType.MESH,
        ),
    )
    for d in range(n):
        lanes = slice(d * ud, (d + 1) * ud)
        upper_stage[d] = rows_of(upper_in, lanes)
        lower_stage[d] = rows_of(lower_in, lanes)
    pl.semaphore_wait(barrier, n - 1)

    def send_first(k):
        copy_to(upper_stage, upper, 0, peer_of(k)).start()
        copy_to(lower_stage, lower, 1, peer_of(k)).start()

    each(1, send_first)
    upper[me] = upper_stage[me]
    lower[me] = lower_stage[me]
    for d in range(n):
        power[d] = rows_of(power_in, slice(d * ud, (d + 1) * ud))
    for j in range(hdev):
        flow[j * scen : (j + 1) * scen, :] = flow_in[:, j, :]
    piece = 128
    names = bus_in[...]
    for b in range(0, buses, piece):
        rows = lax.broadcasted_iota(jnp.int32, (piece, units), 0) + b
        inc[b : b + piece, :] = jnp.where(rows == names, 1.0, 0.0).astype(jnp.bfloat16)
    capacity_out[...] = capacity_in[...]
    retain = 1.0 - leak_in[pl.ds(me, 1), :]
    begin = start_in[pl.ds(me, 1), :]
    cost = cost_in[pl.ds(me, 1), :]
    price = price_in[...]
    load_shift.wait()

    def wait_first(k):
        wait_from(upper, 0, from_of(k))
        wait_from(lower, 1, from_of(k))
        copy_to(upper_stage, upper, 0, peer_of(k)).wait_send()
        copy_to(lower_stage, lower, 1, peer_of(k)).wait_send()

    each(1, wait_first)

    def iteration(step, carry):
        w = jnp.zeros((scen, ud), jnp.float32)
        total = jnp.zeros((scen, ud), jnp.float32)
        for t in reversed(range(hours)):
            d, rows = t // hdev, slice((t % hdev) * scen, (t % hdev + 1) * scen)
            up = upper[d, rows, :]
            w = retain * w + (up - lower[d, rows, :])
            total = total + up
            adj[d, rows, :] = w
        each(1, lambda k: copy_to(adj, adj_got, 2, peer_of(k)).start())
        adj_got[me] = adj[me]
        dual_total = jnp.sum(total, axis=0, keepdims=True)
        capacity = capacity_out[...]
        trial_capacity = jnp.maximum(
            capacity - primal_step * (hours * cost - dual_total / scen), 0.0
        )
        capacity_bar = 2.0 * trial_capacity - capacity
        capacity_out[...] = trial_capacity

        bus_dual = jnp.dot(
            flow[...].astype(jnp.bfloat16), shift[...], preferred_element_type=jnp.float32
        ).astype(jnp.bfloat16)
        grid_grad = jnp.dot(bus_dual, inc[...], preferred_element_type=jnp.float32)
        for d in range(n):
            grid[d] = grid_grad[:, d * ud : (d + 1) * ud]

        def advance(d):
            limit = plimit_in[pl.ds(d, 1), :]
            old = power[d]
            trial = jnp.clip(
                old - primal_step * (grid[d] - adj_got[d] - price), -limit, limit
            )
            bar[d] = 2.0 * trial - old
            power[d] = trial

        advance(me)
        bar_got[me] = bar[me]

        def answer(k):
            source = from_of(k)
            wait_from(adj_got, 2, source)
            advance(source)
            copy_to(bar, bar_got, 3, source).start()

        each(1, answer)
        for d in range(n):
            bar16[:, d * ud : (d + 1) * ud] = bar[d].astype(jnp.bfloat16)
        injection = lax.dot_general(
            bar16[...], inc[...], (((1,), (1,)), ((), ())), preferred_element_type=jnp.float32
        )
        load = jnp.concatenate([load_in[:, j, :] for j in range(hdev)], axis=0)
        injection = (injection - load.astype(jnp.float32)).astype(jnp.bfloat16)
        width = min(1024, lines)
        for c in range(0, lines, width):
            flows = lax.dot_general(
                injection,
                shift[c : c + width, :],
                (((1,), (1,)), ((), ())),
                preferred_element_type=jnp.float32,
            )
            probe = flow[:, c : c + width] + dual_step * flows
            edge = dual_step * limit_in[:, c : c + width]
            flow[:, c : c + width] = probe - jnp.clip(probe, -edge, edge)

        def wait_bar(k):
            wait_from(bar_got, 3, from_of(k))
            copy_to(adj, adj_got, 2, peer_of(k)).wait_send()
            copy_to(bar, bar_got, 3, from_of(k)).wait_send()

        each(1, wait_bar)
        e = jnp.broadcast_to(begin, (scen, ud))
        for t in range(hours):
            d, rows = t // hdev, slice((t % hdev) * scen, (t % hdev + 1) * scen)
            e = retain * e - bar_got[d, rows, :]
            upper[d, rows, :] = jnp.maximum(
                upper[d, rows, :] + dual_step * (e - capacity_bar), 0.0
            )
            lower[d, rows, :] = jnp.maximum(lower[d, rows, :] - dual_step * e, 0.0)
        return carry

    lax.fori_loop(0, ITERS, iteration, 0)

    def send_last(k):
        copy_to(upper, adj_got, 2, peer_of(k)).start()
        copy_to(lower, lower_stage, 0, peer_of(k)).start()

    each(1, send_last)
    adj_got[me] = upper[me]
    lower_stage[me] = lower[me]
    for d in range(n):
        for j in range(hdev):
            power_out[:, j, d * ud : (d + 1) * ud] = power[d, j * scen : (j + 1) * scen, :]
    for j in range(hdev):
        flow_out[:, j, :] = flow[j * scen : (j + 1) * scen, :]

    def wait_last(k):
        wait_from(adj_got, 2, from_of(k))
        wait_from(lower_stage, 0, from_of(k))
        copy_to(upper, adj_got, 2, peer_of(k)).wait_send()
        copy_to(lower, lower_stage, 0, peer_of(k)).wait_send()

    each(1, wait_last)
    for d in range(n):
        for j in range(hdev):
            lanes, rows = slice(d * ud, (d + 1) * ud), slice(j * scen, (j + 1) * scen)
            upper_out[:, j, lanes] = adj_got[d, rows, :]
            lower_out[:, j, lanes] = lower_stage[d, rows, :]


def on_device(
    power,
    capacity,
    flow_dual,
    upper_dual,
    lower_dual,
    price,
    load,
    shift_factors,
    line_limit,
    unit_bus,
    leakage,
    initial_state,
    power_limit,
    capacity_cost,
):
    n = lax.axis_size("hour")
    scen, hdev, units = power.shape
    lines, buses = shift_factors.shape
    ud, rows = units // n, scen * hdev
    block = pltpu.VMEM((n, rows, ud), jnp.float32)
    vmem = pl.BlockSpec(memory_space=pltpu.VMEM)
    anywhere = pl.BlockSpec(memory_space=pl.ANY)
    out = pl.pallas_call(
        functools.partial(kernel, n),
        out_shape=(
            jax.ShapeDtypeStruct(power.shape, jnp.float32),
            jax.ShapeDtypeStruct((1, ud), jnp.float32),
            jax.ShapeDtypeStruct(flow_dual.shape, jnp.float32),
            jax.ShapeDtypeStruct(upper_dual.shape, jnp.float32),
            jax.ShapeDtypeStruct(lower_dual.shape, jnp.float32),
        ),
        in_specs=[vmem] * 7 + [anywhere] + [vmem] * 6,
        out_specs=(vmem,) * 5,
        scratch_shapes=[
            pltpu.VMEM((lines, buses), jnp.bfloat16),
            pltpu.VMEM((buses, units), jnp.bfloat16),
            block,
            block,
            pltpu.VMEM((rows, lines), jnp.float32),
            pltpu.VMEM((rows, units), jnp.bfloat16),
            block,
            block,
            block,
            block,
            block,
            block,
            block,
            block,
            pltpu.SemaphoreType.DMA((4, n)),
            pltpu.SemaphoreType.DMA((4, n)),
            pltpu.SemaphoreType.DMA,
        ],
        compiler_params=pltpu.CompilerParams(
            collective_id=0, has_side_effects=True, vmem_limit_bytes=48 * 1024 * 1024
        ),
    )(
        power,
        capacity.reshape(1, ud),
        flow_dual,
        upper_dual,
        lower_dual,
        price.T.reshape(rows, 1),
        load,
        shift_factors,
        line_limit.reshape(1, lines),
        unit_bus.reshape(1, units),
        leakage.reshape(n, ud),
        initial_state.reshape(n, ud),
        power_limit.reshape(n, ud),
        capacity_cost.reshape(n, ud),
    )
    return (out[0], out[1].reshape(ud), out[2], out[3], out[4])


def solution(mesh):
    return jax.shard_map(
        on_device,
        mesh=mesh,
        in_specs=(
            P("groups", "hour", None),
            P(("groups", "hour")),
            P("groups", "hour", None),
            P("groups", "hour", None),
            P("groups", "hour", None),
            P("groups", "hour"),
            P("groups", "hour", None),
            P(),
            P(),
            P(),
            P(),
            P("groups"),
            P(),
            P(),
        ),
        out_specs=(
            P("groups", "hour", None),
            P(("groups", "hour")),
            P("groups", "hour", None),
            P("groups", "hour", None),
            P("groups", "hour", None),
        ),
        check_vma=False,
    )
```

profile of v0, /device:TPU:0, one launch (start us, length us, event | category | flops | bytes accessed | tf_op | source)
XLA Modules:
  0.0 74.4 jit_solution(5865183582958653938)
XLA Ops:
  0.6 0.7 copy.19.price_in
  1.4 0.7 copy.20.load_in
  2.1 0.0 copy-start
  2.1 2.2 %copy-done = bf16[4096,512]{1,0:T(8,128)(2,1)S(1)} copy-done((bf16[4096,512]{1,0:T(8,128)(2,1)S(1)}, bf16[4096,512]{1,0:T(8,128)(2,1)}, u32[]{:S(2)}) %copy-start) | copy-done | bytes 4194328
  4.3 0.0 copy-start.1
  4.3 0.9 %copy-done.1 = f32[16,1,4096]{2,1,0:T(1,128)S(1)} copy-done((f32[16,1,4096]{2,1,0:T(1,128)S(1)}, f32[16,1,4096]{2,1,0:T(1,128)}, u32[]{:S(2)}) %copy-start.1) | copy-done | bytes 262168
  5.3 0.0 copy-start.2
  5.3 0.9 %copy-done.2 = f32[16,1,2048]{2,1,0:T(1,128)S(1)} copy-done((f32[16,1,2048]{2,1,0:T(1,128)S(1)}, f32[16,1,2048]{2,1,0:T(1,128)}, u32[]{:S(2)}) %copy-start.2) | copy-done | bytes 131096
  6.2 0.0 copy-start.3
  6.2 0.9 %copy-done.3 = f32[16,1,2048]{2,1,0:T(1,128)S(1)} copy-done((f32[16,1,2048]{2,1,0:T(1,128)S(1)}, f32[16,1,2048]{2,1,0:T(1,128)}, u32[]{:S(2)}) %copy-start.3) | copy-done | bytes 131096
  7.1 0.0 copy-start.4
  7.1 0.9 %copy-done.4 = f32[16,1,2048]{2,1,0:T(1,128)S(1)} copy-done((f32[16,1,2048]{2,1,0:T(1,128)S(1)}, f32[16,1,2048]{2,1,0:T(1,128)}, u32[]{:S(2)}) %copy-start.4) | copy-done | bytes 131096
  8.0 0.0 copy-start.5
  8.0 0.7 copy-done.5
  8.7 0.0 copy-start.6
  8.7 0.7 copy-done.6
  9.4 0.0 copy-start.7
  9.4 0.7 copy-done.7
  10.1 0.0 copy-start.8
  10.1 0.7 copy-done.8
  10.8 0.0 copy-start.9
  10.8 0.7 copy-done.9
  11.5 0.0 copy-start.10
  11.5 0.7 copy-done.10
  12.2 0.0 copy-start.11
  12.2 0.7 copy-done.11
  12.8 58.4 %shard_map.173 = (f32[16,1,2048]{2,1,0:T(1,128)S(1)}, f32[1,128]{1,0:T(1,128)S(1)}, f32[16,1,4096]{2,1,0:T(1,128)S(1)}, f32[16,1,2048]{2,1,0:T(1,128)S(1)}, f32[16,1,2048]{2,1,0:T(1,128)S(1)}) custom-call(f32[16,1,2048]{2,1,0:T(1,128)S(1)} %copy-done.2, f32[1,128]{1,0:T(1,128)S(1)} %bitcast.14, f32[16,1,4096]{2,1,0:T(1,128)S(1)} %copy-done.1, ...), custom_call_target="tpu_custom_call" | custom-call | tf_op jit(solution)/shard_map/pallas_call | solution.py:278
  71.3 0.7 copy.26
  71.9 0.5 copy.27
  72.4 0.7 copy.28
  73.1 0.7 copy.29
  73.8 0.7 copy.30
Async XLA Ops:
  2.1 2.2 %copy-start = (bf16[4096,512]{1,0:T(8,128)(2,1)S(1)}, bf16[4096,512]{1,0:T(8,128)(2,1)}, u32[]{:S(2)}) copy-start(bf16[4096,512]{1,0:T(8,128)(2,1)} %shift_in.1) | copy-start | bytes 12582916
  4.3 0.9 %copy-start.1 = (f32[16,1,4096]{2,1,0:T(1,128)S(1)}, f32[16,1,4096]{2,1,0:T(1,128)}, u32[]{:S(2)}) copy-start(f32[16,1,4096]{2,1,0:T(1,128)} %flow_in.1) | copy-start | bytes 786436
  5.3 0.9 %copy-start.2 = (f32[16,1,2048]{2,1,0:T(1,128)S(1)}, f32[16,1,2048]{2,1,0:T(1,128)}, u32[]{:S(2)}) copy-start(f32[16,1,2048]{2,1,0:T(1,128)} %power_in.1) | copy-start | bytes 393220
  6.2 0.9 %copy-start.3 = (f32[16,1,2048]{2,1,0:T(1,128)S(1)}, f32[16,1,2048]{2,1,0:T(1,128)}, u32[]{:S(2)}) copy-start(f32[16,1,2048]{2,1,0:T(1,128)} %upper_in.1) | copy-start | bytes 393220
  7.1 0.9 %copy-start.4 = (f32[16,1,2048]{2,1,0:T(1,128)S(1)}, f32[16,1,2048]{2,1,0:T(1,128)}, u32[]{:S(2)}) copy-start(f32[16,1,2048]{2,1,0:T(1,128)} %lower_in.1) | copy-start | bytes 393220
  8.0 0.7 copy-start.5
  8.7 0.7 copy-start.6
  9.4 0.7 copy-start.7
  10.1 0.7 copy-start.8
  10.8 0.7 copy-start.9
  11.5 0.7 copy-start.10
  12.2 0.7 copy-start.11
where the time goes:
time: 75.1 us; the launch traced here: 74.4 us
  Pallas kernels  58.4 us (78%)
  local copies, waits for them, and re-layouts  15.4 us (21%)
    pallas_call x1, Pallas kernels, on_device(): pl.pallas_call(functools.partial(kernel, n), out_shape=(jax.ShapeDtypeStr...  58.4 us
    unnamed x31, local copies, waits for them, and re-layouts  15.4 us

commit v1 on v0

--- a/solution.py
+++ b/solution.py
@@ -13,52 +13,56 @@
 dual_step = 0.01
 
 
-def kernel(
-    n,
-    power_in,
-    capacity_in,
-    flow_in,
-    upper_in,
-    lower_in,
-    price_in,
-    load_in,
-    shift_in,
-    limit_in,
-    bus_in,
-    leak_in,
-    start_in,
-    plimit_in,
-    cost_in,
-    power_out,
-    capacity_out,
-    flow_out,
-    upper_out,
-    lower_out,
-    shift,
-    inc,
-    power,
-    grid,
-    flow,
-    bar16,
-    upper,
-    lower,
-    upper_stage,
-    lower_stage,
-    adj,
-    adj_got,
-    bar,
-    bar_got,
-    send_sems,
-    recv_sems,
-    shift_sem,
-):
+def kernel(n, *refs):
+    arrived, refs = refs[:14], refs[14:]
+    (power_out, capacity_out, flow_out, upper_out, lower_out), refs = refs[:5], refs[5:]
+    held, refs = refs[:14], refs[14:]
+    (
+        power_in,
+        capacity_in,
+        flow_in,
+        upper_in,
+        lower_in,
+        price_in,
+        load_in,
+        shift,
+        limit_in,
+        bus_in,
+        leak_in,
+        start_in,
+        plimit_in,
+        cost_in,
+    ) = held
+    (
+        inc,
+        power,
+        grid,
+        flow,
+        bar16,
+        upper,
+        lower,
+        upper_stage,
+        lower_stage,
+        adj,
+        adj_got,
+        bar,
+        bar_got,
+        send_sems,
+        recv_sems,
+        load_sems,
+    ) = refs
     me = lax.axis_index("hour")
     scen, hdev, units = power_in.shape
     lines, buses = shift.shape
     ud = units // n
     hours = hdev * n
-    load_shift = pltpu.make_async_copy(shift_in, shift, shift_sem)
-    load_shift.start()
+    loads = [
+        pltpu.make_async_copy(src, dst, load_sems.at[i])
+        for i, (src, dst) in enumerate(zip(arrived, held))
+    ]
+    first = (3, 4)
+    for i in first:
+        loads[i].start()
 
     def peer_of(k):
         return lax.rem(me + k, n)
@@ -106,6 +110,10 @@
             device_id_type=pl.DeviceIdType.MESH,
         ),
     )
+    for i in (9, 0, 2, 7, 1, 5, 6, 8, 10, 11, 12, 13):
+        loads[i].start()
+    for i in first:
+        loads[i].wait()
     for d in range(n):
         lanes = slice(d * ud, (d + 1) * ud)
         upper_stage[d] = rows_of(upper_in, lanes)
@@ -119,6 +127,9 @@
     each(1, send_first)
     upper[me] = upper_stage[me]
     lower[me] = lower_stage[me]
+    for i in range(14):
+        if i not in first and i != 7:
+            loads[i].wait()
     for d in range(n):
         power[d] = rows_of(power_in, slice(d * ud, (d + 1) * ud))
     for j in range(hdev):
@@ -132,8 +143,17 @@
     retain = 1.0 - leak_in[pl.ds(me, 1), :]
     begin = start_in[pl.ds(me, 1), :]
     cost = cost_in[pl.ds(me, 1), :]
-    price = price_in[...]
-    load_shift.wait()
+    eye = lax.broadcasted_iota(jnp.int32, (scen, scen), 0) == lax.broadcasted_iota(
+        jnp.int32, (scen, scen), 1
+    )
+    price = jnp.concatenate(
+        [
+            jnp.sum(jnp.where(eye, price_in[j : j + 1, :], 0.0), axis=1, keepdims=True)
+            for j in range(hdev)
+        ],
+        axis=0,
+    )
+    loads[7].wait()
 
     def wait_first(k):
         wait_from(upper, 0, from_of(k))
@@ -193,7 +213,7 @@
         injection = lax.dot_general(
             bar16[...], inc[...], (((1,), (1,)), ((), ())), preferred_element_type=jnp.float32
         )
-        load = jnp.concatenate([load_in[:, j, :] for j in range(hdev)], axis=0)
+        load = jnp.concatenate([load_in[j] for j in range(hdev)], axis=0)
         injection = (injection - load.astype(jnp.float32)).astype(jnp.bfloat16)
         width = min(1024, lines)
         for c in range(0, lines, width):
@@ -250,6 +270,17 @@
             lanes, rows = slice(d * ud, (d + 1) * ud), slice(j * scen, (j + 1) * scen)
             upper_out[:, j, lanes] = adj_got[d, rows, :]
             lower_out[:, j, lanes] = lower_stage[d, rows, :]
+
+
+def store(*refs):
+    sems = refs[10]
+    copies = [
+        pltpu.make_async_copy(refs[i], refs[5 + i], sems.at[i]) for i in (2, 0, 3, 4, 1)
+    ]
+    for copy in copies:
+        copy.start()
+    for copy in copies:
+        copy.wait()
 
 
 def on_device(
@@ -274,48 +305,15 @@
     ud, rows = units // n, scen * hdev
     block = pltpu.VMEM((n, rows, ud), jnp.float32)
     vmem = pl.BlockSpec(memory_space=pltpu.VMEM)
-    anywhere = pl.BlockSpec(memory_space=pl.ANY)
-    out = pl.pallas_call(
-        functools.partial(kernel, n),
-        out_shape=(
-            jax.ShapeDtypeStruct(power.shape, jnp.float32),
-            jax.ShapeDtypeStruct((1, ud), jnp.float32),
-            jax.ShapeDtypeStruct(flow_dual.shape, jnp.float32),
-            jax.ShapeDtypeStruct(upper_dual.shape, jnp.float32),
-            jax.ShapeDtypeStruct(lower_dual.shape, jnp.float32),
-        ),
-        in_specs=[vmem] * 7 + [anywhere] + [vmem] * 6,
-        out_specs=(vmem,) * 5,
-        scratch_shapes=[
-            pltpu.VMEM((lines, buses), jnp.bfloat16),
-            pltpu.VMEM((buses, units), jnp.bfloat16),
-            block,
-            block,
-            pltpu.VMEM((rows, lines), jnp.float32),
-            pltpu.VMEM((rows, units), jnp.bfloat16),
-            block,
-            block,
-            block,
-            block,
-            block,
-            block,
-            block,
-            block,
-            pltpu.SemaphoreType.DMA((4, n)),
-            pltpu.SemaphoreType.DMA((4, n)),
-            pltpu.SemaphoreType.DMA,
-        ],
-        compiler_params=pltpu.CompilerParams(
-            collective_id=0, has_side_effects=True, vmem_limit_bytes=48 * 1024 * 1024
-        ),
-    )(
+    hbm = pl.BlockSpec(memory_space=pltpu.HBM)
+    args = (
         power,
         capacity.reshape(1, ud),
         flow_dual,
         upper_dual,
         lower_dual,
-        price.T.reshape(rows, 1),
-        load,
+        price.T,
+        load.transpose(1, 0, 2),
         shift_factors,
         line_limit.reshape(1, lines),
         unit_bus.reshape(1, units),
@@ -324,6 +322,40 @@
         power_limit.reshape(n, ud),
         capacity_cost.reshape(n, ud),
     )
+    results = tuple(
+        jax.ShapeDtypeStruct(args[i].shape, jnp.float32) for i in range(5)
+    )
+    out = pl.pallas_call(
+        functools.partial(kernel, n),
+        out_shape=results,
+        in_specs=[hbm] * 14,
+        out_specs=(vmem,) * 5,
+        scratch_shapes=[pltpu.VMEM(a.shape, a.dtype) for a in args]
+        + [
+            pltpu.VMEM((buses, units), jnp.bfloat16),
+            block,
+            block,
+            pltpu.VMEM((rows, lines), jnp.float32),
+            pltpu.VMEM((rows, units), jnp.bfloat16),
+        ]
+        + [block] * 8
+        + [
+            pltpu.SemaphoreType.DMA((4, n)),
+            pltpu.SemaphoreType.DMA((4, n)),
+            pltpu.SemaphoreType.DMA((14,)),
+        ],
+        compiler_params=pltpu.CompilerParams(
+            collective_id=0, has_side_effects=True, vmem_limit_bytes=48 * 1024 * 1024
+        ),
+    )(*(pltpu.with_memory_space_constraint(a, pltpu.HBM) for a in args))
+    out = pl.pallas_call(
+        store,
+        out_shape=results,
+        in_specs=[vmem] * 5,
+        out_specs=(hbm,) * 5,
+        scratch_shapes=[pltpu.SemaphoreType.DMA((5,))],
+        compiler_params=pltpu.CompilerParams(vmem_limit_bytes=16 * 1024 * 1024),
+    )(*out)
     return (out[0], out[1].reshape(ud), out[2], out[3], out[4])
 
 

time: 75.1 us -> 60 us (0.80)
  local copies, waits for them, and re-layouts: 15.4 us -> 0 us
  Pallas kernels: 58.4 us -> 59.2 us
    unnamed x31 -> x0, local copies, waits for them, and re-layouts: 15.4 us -> none
    pallas_call x1 -> x2, Pallas kernels: 58.4 us -> 59.2 us  [the longest x1 58.3 us: on_device(): pl.pallas_call(functools.partial(kernel, n), out_shape=results, in_specs=...]
where the time goes in v1:
time: 60 us; the launch traced here: 59.8 us
  Pallas kernels  59.2 us (99%)
  between operations  0.65 us (1%)
    pallas_call x1, Pallas kernels, on_device(): pl.pallas_call(functools.partial(kernel, n), out_shape=results, in_specs=...  58.3 us

profile of v1, /device:TPU:0, one launch (start us, length us, event | category | flops | bytes accessed | tf_op | source)
XLA Modules:
  0.0 59.8 jit_solution(9206030613423218286)
XLA Ops:
  0.6 58.3 %shard_map.173 = (f32[16,1,2048]{2,1,0:T(1,128)S(1)}, f32[1,128]{1,0:T(1,128)S(1)}, f32[16,1,4096]{2,1,0:T(1,128)S(1)}, f32[16,1,2048]{2,1,0:T(1,128)S(1)}, f32[16,1,2048]{2,1,0:T(1,128)S(1)}) custom-call(f32[16,1,2048]{2,1,0:T(1,128)} %refs_0_.1, f32[1,128]{1,0:T(1,128)} %bitcast.17, f32[16,1,4096]{2,1,0:T(1,128)} %refs_2_.1, f32[16,1,2048]{2,1,0:T(1,128)} %refs_3_.1, ...), custom_call_target="tpu_custom_call" | custom-call | tf_op jit(solution)/shard_map/pallas_call | solution.py:328
  59.0 0.9 %shard_map.174 = (f32[16,1,2048]{2,1,0:T(1,128)}, f32[1,128]{1,0:T(1,128)}, f32[16,1,4096]{2,1,0:T(1,128)}, f32[16,1,2048]{2,1,0:T(1,128)}, f32[16,1,2048]{2,1,0:T(1,128)}) custom-call(f32[16,1,2048]{2,1,0:T(1,128)S(1)} %get-tuple-element.15.refs_0_, f32[1,128]{1,0:T(1,128)S(1)} %get-tuple-element.16.refs_1_, f32[16,1,4096]{2,1,0:T(1,128)S(1)} %get-tuple-element.17.refs_2_, ...), custom_call_target="tpu_custom_call" | custom-call | tf_op jit(solution)/shard_map/pallas_call | solution.py:351

commit v2 on v1

--- a/solution.py
+++ b/solution.py
@@ -65,10 +65,7 @@
         loads[i].start()
 
     def peer_of(k):
-        return lax.rem(me + k, n)
-
-    def from_of(k):
-        return lax.rem(me + n - k, n)
+        return me ^ k
 
     def copy_to(src, dst, channel, peer):
         return pltpu.make_async_remote_copy(
@@ -90,19 +87,20 @@
             device_id_type=pl.DeviceIdType.MESH,
         ).wait_recv()
 
-    def each(count_from, function):
-        def step(k, carry):
+    blocks = sorted(range(1, n // 4), key=lambda z: -min(z, n // 4 - z))
+    order = [z * 4 + low for low in (2, 3, 0, 1) for z in blocks] + [2, 3, 1]
+    assert n % 4 == 0 and n & (n - 1) == 0 and sorted(order) == list(range(1, n))
+
+    def each(order, function):
+        for k in order:
             function(k)
-            return carry
-
-        lax.fori_loop(count_from, n, step, 0)
 
     def rows_of(ref, lanes):
         return jnp.concatenate([ref[:, j, lanes] for j in range(hdev)], axis=0)
 
     barrier = pltpu.get_barrier_semaphore()
     each(
-        1,
+        order,
         lambda k: pl.semaphore_signal(
             barrier,
             inc=1,
@@ -117,14 +115,11 @@
     for d in range(n):
         lanes = slice(d * ud, (d + 1) * ud)
         upper_stage[d] = rows_of(upper_in, lanes)
-        lower_stage[d] = rows_of(lower_in, lanes)
+        lower_stage[d] = upper_stage[d] - rows_of(lower_in, lanes)
     pl.semaphore_wait(barrier, n - 1)
 
-    def send_first(k):
-        copy_to(upper_stage, upper, 0, peer_of(k)).start()
-        copy_to(lower_stage, lower, 1, peer_of(k)).start()
-
-    each(1, send_first)
+    each(order, lambda k: copy_to(lower_stage, lower, 1, peer_of(k)).start())
+    each(order, lambda k: copy_to(upper_stage, upper, 0, peer_of(k)).start())
     upper[me] = upper_stage[me]
     lower[me] = lower_stage[me]
     for i in range(14):
@@ -155,33 +150,19 @@
     )
     loads[7].wait()
 
-    def wait_first(k):
-        wait_from(upper, 0, from_of(k))
-        wait_from(lower, 1, from_of(k))
-        copy_to(upper_stage, upper, 0, peer_of(k)).wait_send()
-        copy_to(lower_stage, lower, 1, peer_of(k)).wait_send()
-
-    each(1, wait_first)
-
-    def iteration(step, carry):
+    def place(t):
+        return t // hdev, slice((t % hdev) * scen, (t % hdev + 1) * scen)
+
+    def adjoint(difference):
         w = jnp.zeros((scen, ud), jnp.float32)
-        total = jnp.zeros((scen, ud), jnp.float32)
         for t in reversed(range(hours)):
-            d, rows = t // hdev, slice((t % hdev) * scen, (t % hdev + 1) * scen)
-            up = upper[d, rows, :]
-            w = retain * w + (up - lower[d, rows, :])
-            total = total + up
+            d, rows = place(t)
+            w = retain * w + difference(d, rows)
             adj[d, rows, :] = w
-        each(1, lambda k: copy_to(adj, adj_got, 2, peer_of(k)).start())
+        each(order, lambda k: copy_to(adj, adj_got, 2, peer_of(k)).start())
         adj_got[me] = adj[me]
-        dual_total = jnp.sum(total, axis=0, keepdims=True)
-        capacity = capacity_out[...]
-        trial_capacity = jnp.maximum(
-            capacity - primal_step * (hours * cost - dual_total / scen), 0.0
-        )
-        capacity_bar = 2.0 * trial_capacity - capacity
-        capacity_out[...] = trial_capacity
-
+
+    def iteration(first):
         bus_dual = jnp.dot(
             flow[...].astype(jnp.bfloat16), shift[...], preferred_element_type=jnp.float32
         ).astype(jnp.bfloat16)
@@ -202,12 +183,12 @@
         bar_got[me] = bar[me]
 
         def answer(k):
-            source = from_of(k)
+            source = peer_of(k)
             wait_from(adj_got, 2, source)
             advance(source)
             copy_to(bar, bar_got, 3, source).start()
 
-        each(1, answer)
+        each(order, answer)
         for d in range(n):
             bar16[:, d * ud : (d + 1) * ud] = bar[d].astype(jnp.bfloat16)
         injection = lax.dot_general(
@@ -227,29 +208,59 @@
             edge = dual_step * limit_in[:, c : c + width]
             flow[:, c : c + width] = probe - jnp.clip(probe, -edge, edge)
 
+        if first:
+
+            def wait_upper(k):
+                wait_from(upper, 0, peer_of(k))
+                copy_to(upper_stage, upper, 0, peer_of(k)).wait_send()
+                copy_to(lower_stage, lower, 1, peer_of(k)).wait_send()
+
+            each(order, wait_upper)
+            for d in range(n):
+                lower[d] = upper[d] - lower[d]
+        total = jnp.zeros((scen, ud), jnp.float32)
+        for t in range(hours):
+            d, rows = place(t)
+            total = total + upper[d, rows, :]
+        dual_total = jnp.sum(total, axis=0, keepdims=True)
+        capacity = capacity_out[...]
+        trial_capacity = jnp.maximum(
+            capacity - primal_step * (hours * cost - dual_total / scen), 0.0
+        )
+        capacity_bar = 2.0 * trial_capacity - capacity
+        capacity_out[...] = trial_capacity
+
         def wait_bar(k):
-            wait_from(bar_got, 3, from_of(k))
+            wait_from(bar_got, 3, peer_of(k))
             copy_to(adj, adj_got, 2, peer_of(k)).wait_send()
-            copy_to(bar, bar_got, 3, from_of(k)).wait_send()
-
-        each(1, wait_bar)
+            copy_to(bar, bar_got, 3, peer_of(k)).wait_send()
+
+        each(order, wait_bar)
         e = jnp.broadcast_to(begin, (scen, ud))
         for t in range(hours):
-            d, rows = t // hdev, slice((t % hdev) * scen, (t % hdev + 1) * scen)
+            d, rows = place(t)
             e = retain * e - bar_got[d, rows, :]
             upper[d, rows, :] = jnp.maximum(
                 upper[d, rows, :] + dual_step * (e - capacity_bar), 0.0
             )
             lower[d, rows, :] = jnp.maximum(lower[d, rows, :] - dual_step * e, 0.0)
+
+    each(order, lambda k: wait_from(lower, 1, peer_of(k)))
+    adjoint(lambda d, rows: lower[d, rows, :])
+    iteration(True)
+
+    def again(step, carry):
+        adjoint(lambda d, rows: upper[d, rows, :] - lower[d, rows, :])
+        iteration(False)
         return carry
 
-    lax.fori_loop(0, ITERS, iteration, 0)
+    lax.fori_loop(1, ITERS, again, 0)
 
     def send_last(k):
         copy_to(upper, adj_got, 2, peer_of(k)).start()
         copy_to(lower, lower_stage, 0, peer_of(k)).start()
 
-    each(1, send_last)
+    each(order, send_last)
     adj_got[me] = upper[me]
     lower_stage[me] = lower[me]
     for d in range(n):
@@ -259,12 +270,12 @@
         flow_out[:, j, :] = flow[j * scen : (j + 1) * scen, :]
 
     def wait_last(k):
-        wait_from(adj_got, 2, from_of(k))
-        wait_from(lower_stage, 0, from_of(k))
+        wait_from(adj_got, 2, peer_of(k))
+        wait_from(lower_stage, 0, peer_of(k))
         copy_to(upper, adj_got, 2, peer_of(k)).wait_send()
         copy_to(lower, lower_stage, 0, peer_of(k)).wait_send()
 
-    each(1, wait_last)
+    each(order, wait_last)
     for d in range(n):
         for j in range(hdev):
             lanes, rows = slice(d * ud, (d + 1) * ud), slice(j * scen, (j + 1) * scen)

time: 60 us -> 56.4 us (0.940)
  Pallas kernels: 59.2 us -> 55.5 us
    pallas_call x1, Pallas kernels: 58.3 us -> 54.7 us  [on_device(): pl.pallas_call(functools.partial(kernel, n), out_shape=results, in_specs=...]
where the time goes in v2:
time: 56.4 us; the launch traced here: 56.2 us
  Pallas kernels  55.5 us (98%)
  between operations  0.65 us (1%)
    pallas_call x1, Pallas kernels, on_device(): pl.pallas_call(functools.partial(kernel, n), out_shape=results, in_specs=...  54.7 us

profile of v2, /device:TPU:0, one launch (start us, length us, event | category | flops | bytes accessed | tf_op | source)
XLA Modules:
  0.0 56.2 jit_solution(2776622051834875410)
XLA Ops:
  0.6 54.7 %shard_map.173 = (f32[16,1,2048]{2,1,0:T(1,128)S(1)}, f32[1,128]{1,0:T(1,128)S(1)}, f32[16,1,4096]{2,1,0:T(1,128)S(1)}, f32[16,1,2048]{2,1,0:T(1,128)S(1)}, f32[16,1,2048]{2,1,0:T(1,128)S(1)}) custom-call(f32[16,1,2048]{2,1,0:T(1,128)} %refs_0_.1, f32[1,128]{1,0:T(1,128)} %bitcast.17, f32[16,1,4096]{2,1,0:T(1,128)} %refs_2_.1, f32[16,1,2048]{2,1,0:T(1,128)} %refs_3_.1, ...), custom_call_target="tpu_custom_call" | custom-call | tf_op jit(solution)/shard_map/pallas_call | solution.py:339
  55.3 0.9 %shard_map.174 = (f32[16,1,2048]{2,1,0:T(1,128)}, f32[1,128]{1,0:T(1,128)}, f32[16,1,4096]{2,1,0:T(1,128)}, f32[16,1,2048]{2,1,0:T(1,128)}, f32[16,1,2048]{2,1,0:T(1,128)}) custom-call(f32[16,1,2048]{2,1,0:T(1,128)S(1)} %get-tuple-element.15.refs_0_, f32[1,128]{1,0:T(1,128)S(1)} %get-tuple-element.16.refs_1_, f32[16,1,4096]{2,1,0:T(1,128)S(1)} %get-tuple-element.17.refs_2_, ...), custom_call_target="tpu_custom_call" | custom-call | tf_op jit(solution)/shard_map/pallas_call | solution.py:362
